TPU v7x, 256 devices: a whole 4x4x8 slice. The times are simulated.
256 devices in a mesh: span: 8 (over z_lo, y), ulysses: 32 (over x, z_hi, core).
Axes of the slice: x: 4, y: 4, z: 8 (z_hi: 4, z_lo: 2; z = z_hi * 2 + z_lo), core: 2. Of those that a mesh axis runs over, the one named last changes fastest.
Arguments:
- query: bfloat16 [32768, 4096], P(('span', 'ulysses')), may hold values from -32 to 32
- key: bfloat16 [32768, 1024], P(('span', 'ulysses')), may hold values from -6 to 6
- value: bfloat16 [32768, 1024], P(('span', 'ulysses')), may hold values from -6 to 6
- d_out: bfloat16 [32768, 4096], P(('span', 'ulysses')), may hold values from -6 to 6
Outputs:
- attended: bfloat16 [32768, 4096], P(('span', 'ulysses'))
- grad_query: float32 [1024, 4096], P(('span', 'ulysses'))
- grad_key: float32 [1024, 1024], P(('span', 'ulysses'))
- grad_value: float32 [1024, 1024], P(('span', 'ulysses'))
All inputs are finite; a program needn't handle non-finite values.
Results may differ from a plain program's by a relative error of at most 0.0048.
Values may be sent and summed in bfloat16 or wider, within the bound.
A program may use at most 256 MiB of HBM per device.

v0:
```python
import math
import jax
import jax.numpy as jnp
from jax import lax
from jax.sharding import PartitionSpec as P

H = 32
HD = 128
KVH = 8
INTERVAL = 32


def widen(field):
    count = field.shape[0]
    repeat = H // KVH
    spread = jnp.broadcast_to(field.reshape(count, KVH, 1, HD), (count, KVH, repeat, HD))
    return spread.reshape(count, H * HD)


def on_device(query, key, value, d_out):
    tok_rows = query.shape[0]
    n_heads_axis = lax.axis_size("ulysses")
    span_len = tok_rows * n_heads_axis
    per_dev = H // n_heads_axis
    beacons = span_len // INTERVAL
    beacon_dev = tok_rows // INTERVAL
    scale = 1.0 / math.sqrt(HD)
    q_h, k_h, v_h, g_h = (
        lax.all_to_all(query, "ulysses", split_axis=1, concat_axis=0, tiled=True),
        lax.all_to_all(widen(key), "ulysses", split_axis=1, concat_axis=0, tiled=True),
        lax.all_to_all(widen(value), "ulysses", split_axis=1, concat_axis=0, tiled=True),
        lax.all_to_all(d_out, "ulysses", split_axis=1, concat_axis=0, tiled=True),
    )
    own_k = k_h.reshape(beacons, INTERVAL, per_dev * HD)[:, -1]
    own_v = v_h.reshape(beacons, INTERVAL, per_dev * HD)[:, -1]
    prior_k, prior_v = (
        lax.all_gather(own_k, "span", axis=0, tiled=True),
        lax.all_gather(own_v, "span", axis=0, tiled=True),
    )
    all_beacons = prior_k.shape[0]
    mine = lax.axis_index("span")
    visible = jnp.arange(all_beacons) // beacons < mine
    q3 = q_h.reshape(span_len, per_dev, HD)
    k3 = k_h.reshape(span_len, per_dev, HD)
    v3 = v_h.reshape(span_len, per_dev, HD)
    g3 = g_h.reshape(span_len, per_dev, HD)
    pk3 = prior_k.reshape(all_beacons, per_dev, HD)
    pv3 = prior_v.reshape(all_beacons, per_dev, HD)
    own_v3 = v3.reshape(beacons, INTERVAL, per_dev, HD)[:, -1]
    dk_prior = jnp.zeros((all_beacons, per_dev, HD), jnp.float32)
    dv_prior = jnp.zeros((all_beacons, per_dev, HD), jnp.float32)
    dk_own = jnp.zeros((beacons, per_dev, HD), jnp.float32)
    dv_own = jnp.zeros((beacons, per_dev, HD), jnp.float32)
    out_blocks = []
    dq_blocks = []
    block = min(512, span_len)
    n_rows = block // INTERVAL
    for index in range(span_len // block):
        first = index * block
        upper = first + block
        q_blk = q3[first:upper]
        g_blk = g3[first:upper]
        k_loc = k3[:upper]
        v_loc = v3[:upper]
        s_prior = jnp.einsum("qhd,khd->hqk", q_blk, pk3, preferred_element_type=jnp.float32) * scale
        s_prior = jnp.where(visible[None, None, :], s_prior, -jnp.inf)
        s_local = (
            jnp.einsum("qhd,khd->hqk", q_blk, k_loc, preferred_element_type=jnp.float32) * scale
        )
        causal = jnp.arange(upper)[None, :] <= (first + jnp.arange(block))[:, None]
        s_local = jnp.where(causal[None], s_local, -jnp.inf)
        peak = jnp.maximum(jnp.max(s_prior, axis=2), jnp.max(s_local, axis=2))
        e_prior = jnp.exp(s_prior - peak[:, :, None])
        e_local = jnp.exp(s_local - peak[:, :, None])
        denom = jnp.sum(e_prior, axis=2) + jnp.sum(e_local, axis=2)
        p_prior = e_prior / denom[:, :, None]
        p_local = e_local / denom[:, :, None]
        b_prior = p_prior.astype(jnp.bfloat16)
        b_local = p_local.astype(jnp.bfloat16)
        attended = jnp.einsum("hqk,khd->qhd", b_prior, pv3, preferred_element_type=jnp.float32)
        attended = attended + jnp.einsum(
            "hqk,khd->qhd", b_local, v_loc, preferred_element_type=jnp.float32
        )
        out_b = attended.astype(jnp.bfloat16)
        out_blocks.append(out_b)
        delta = jnp.sum(g_blk.astype(jnp.float32) * out_b.astype(jnp.float32), axis=2).T
        dp_prior = jnp.einsum("qhd,khd->hqk", g_blk, pv3, preferred_element_type=jnp.float32)
        ds_prior = (p_prior * (dp_prior - delta[:, :, None])).astype(jnp.bfloat16)
        dk_prior = (
            dk_prior
            + jnp.einsum("hqk,qhd->khd", ds_prior, q_blk, preferred_element_type=jnp.float32)
            * scale
        )
        dv_prior = dv_prior + jnp.einsum(
            "hqk,qhd->khd", b_prior, g_blk, preferred_element_type=jnp.float32
        )
        n_own = upper // INTERVAL
        p_own = p_local.reshape(per_dev, block, n_own, INTERVAL)[..., -1]
        b_own = b_local.reshape(per_dev, block, n_own, INTERVAL)[..., -1]
        dp_own = jnp.einsum(
            "qhd,khd->hqk", g_blk, own_v3[:n_own], preferred_element_type=jnp.float32
        )
        ds_own = (p_own * (dp_own - delta[:, :, None])).astype(jnp.bfloat16)
        dk_own = dk_own.at[:n_own].add(
            jnp.einsum("hqk,qhd->khd", ds_own, q_blk, preferred_element_type=jnp.float32) * scale
        )
        dv_own = dv_own.at[:n_own].add(
            jnp.einsum("hqk,qhd->khd", b_own, g_blk, preferred_element_type=jnp.float32)
        )
        ds_rows_prior = ds_prior.reshape(per_dev, n_rows, INTERVAL, all_beacons)[:, :, -1]
        p_rows_local = p_local.reshape(per_dev, n_rows, INTERVAL, upper)[:, :, -1]
        g_rows = g_blk.reshape(n_rows, INTERVAL, per_dev, HD)[:, -1]
        delta_rows = delta.reshape(per_dev, n_rows, INTERVAL)[:, :, -1]
        dp_rows = jnp.einsum("qhd,khd->hqk", g_rows, v_loc, preferred_element_type=jnp.float32)
        ds_rows_local = (p_rows_local * (dp_rows - delta_rows[:, :, None])).astype(jnp.bfloat16)
        dq_rows = jnp.einsum("hqk,khd->qhd", ds_rows_prior, pk3, preferred_element_type=jnp.float32)
        dq_rows = dq_rows + jnp.einsum(
            "hqk,khd->qhd", ds_rows_local, k_loc, preferred_element_type=jnp.float32
        )
        dq_blocks.append(dq_rows * scale)
    out_heads = jnp.concatenate(out_blocks, 0).reshape(span_len, per_dev * HD)
    attended_tokens = lax.all_to_all(out_heads, "ulysses", split_axis=0, concat_axis=1, tiled=True)
    stacked = jnp.stack(
        [dk_prior.reshape(all_beacons, per_dev * HD), dv_prior.reshape(all_beacons, per_dev * HD)],
        1,
    )
    from_later = lax.psum_scatter(stacked, "span", scatter_dimension=0, tiled=True)
    grad_k_heads = dk_own.reshape(beacons, per_dev * HD) + from_later[:, 0]
    grad_v_heads = dv_own.reshape(beacons, per_dev * HD) + from_later[:, 1]
    grad_q_heads = jnp.concatenate(dq_blocks, 0).reshape(beacons, per_dev * HD)
    grad_q_tok, grad_k_tok, grad_v_tok = (
        lax.all_to_all(grad_q_heads, "ulysses", split_axis=0, concat_axis=1, tiled=True),
        lax.all_to_all(grad_k_heads, "ulysses", split_axis=0, concat_axis=1, tiled=True),
        lax.all_to_all(grad_v_heads, "ulysses", split_axis=0, concat_axis=1, tiled=True),
    )
    repeat = H // KVH
    grad_k_tok = (
        grad_k_tok.reshape(beacon_dev, KVH, repeat, HD).sum(axis=2).reshape(beacon_dev, KVH * HD)
    )
    grad_v_tok = (
        grad_v_tok.reshape(beacon_dev, KVH, repeat, HD).sum(axis=2).reshape(beacon_dev, KVH * HD)
    )
    return (attended_tokens, grad_q_tok, grad_k_tok, grad_v_tok)


def solution(mesh):
    return jax.shard_map(
        on_device,
        mesh=mesh,
        in_specs=(
            P(("span", "ulysses"), None),
            P(("span", "ulysses"), None),
            P(("span", "ulysses"), None),
            P(("span", "ulysses"), None),
        ),
        out_specs=(
            P(("span", "ulysses"), None),
            P(("span", "ulysses"), None),
            P(("span", "ulysses"), None),
            P(("span", "ulysses"), None),
        ),
        check_vma=False,
    )
```

profile of v0, /device:TPU:9, one launch (start us, length us, event | category | flops | bytes accessed | tf_op | source)
XLA Modules:
  0.0 729.1 jit_solution(17974472516163867103)
XLA Ops:
  9.4 11.8 %all-to-all-start.2 = ((bf16[128,32,128]{2,0,1:T(8,128)(2,1)}), bf16[128,32,128]{2,0,1:T(8,128)(2,1)S(1)}, u32[]{:S(2)}, u32[]{:S(2)}) async-start(bf16[128,32,128]{2,0,1:T(8,128)(2,1)} %bitcast.8), calls=%async_computation.2 | async-start | bytes 2097152 | tf_op jit(solution)/shard_map/all_to_all | solution.py:31
  21.2 28.5 %all-to-all-done.2 = bf16[128,32,128]{2,0,1:T(8,128)(2,1)S(1)} async-done(((bf16[128,32,128]{2,0,1:T(8,128)(2,1)}), bf16[128,32,128]{2,0,1:T(8,128)(2,1)S(1)}, u32[]{:S(2)}, u32[]{:S(2)}) %all-to-all-start.2) | async-done | bytes 1048608 | tf_op jit(solution)/shard_map/all_to_all | solution.py:31
  51.0 4.9 all-to-all-start.1
  58.2 26.2 %all-to-all-done.1 = bf16[128,32,128]{2,0,1:T(8,128)(2,1)S(1)} async-done(((bf16[128,32,128]{2,0,1:T(8,128)(2,1)}), bf16[128,32,128]{2,0,1:T(8,128)(2,1)S(1)}, u32[]{:S(2)}, u32[]{:S(2)}) %all-to-all-start.1) | async-done | bytes 1048608 | tf_op jit(solution)/shard_map/all_to_all | solution.py:30
  84.3 5.3 all-to-all-start
  95.7 35.9 %all-gather.1 = bf16[1024,1,128]{2,0,1:T(8,128)(2,1)S(1)} all-gather(bf16[128,1,128]{2,0,1:T(8,128)(2,1)S(1)} %copy.230), channel_id=3, replica_groups=mesh['span'=8,'ulysses'=32] {'span'}, dimensions={0}, use_global_device_ids=true | all-gather | bytes 294912 | tf_op jit(solution)/shard_map/all_gather | solution.py:38
  131.6 14.3 %all-to-all-start.4 = ((bf16[128,32,128]{0,2,1:T(8,128)(2,1)}), bf16[128,32,128]{0,2,1:T(8,128)(2,1)}, u32[]{:S(2)}, u32[]{:S(2)}) async-start(bf16[128,32,128]{0,2,1:T(8,128)(2,1)} %bitcast.868), calls=%async_computation.4 | async-start | bytes 2097152 | tf_op jit(solution)/shard_map/all_to_all | solution.py:32
  150.3 37.2 %all-gather = bf16[1024,1,128]{2,0,1:T(8,128)(2,1)S(1)} all-gather(bf16[128,1,128]{2,0,1:T(8,128)(2,1)S(1)} %copy.228), channel_id=2, replica_groups=mesh['span'=8,'ulysses'=32] {'span'}, dimensions={0}, use_global_device_ids=true | all-gather | bytes 294912 | tf_op jit(solution)/shard_map/all_gather | solution.py:37
  214.7 2.7 fusion.265
  228.3 3.0 slice_convert_fusion
  236.6 6.8 fusion.34
  249.1 3.3 fusion.399
  252.5 3.9 fusion.398
  256.4 4.3 fusion.397
  260.8 5.8 fusion.396
  268.4 5.1 fusion.28
  275.9 3.3 fusion.41
  285.9 4.8 fusion.388
  290.7 3.5 fusion.386
  329.3 4.0 fusion.7
  333.3 4.5 fusion.5
  337.8 4.8 fusion.3
  362.0 7.3 %fusion.384 = (bf16[512,2560]{1,0:T(8,128)(2,1)}, f32[512,2560]{1,0:T(8,128)}) fusion(f32[512]{0:T(512)S(1)} %add.460, f32[512,2560]{1,0:T(8,128)} %get-tuple-element.287, f32[512]{0:T(512)} %copy-done.118), kind=kLoop, calls=%fused_computation.511 | loop fusion | flops 3932160 | bytes 13111296 | tf_op jit(solution)/shard_map/convert_element_type | solution.py:79
  369.4 5.3 fusion.382
  375.0 5.7 fusion.380
  380.9 7.2 fusion.378
  389.8 5.6 fusion.390
  404.4 3.2 multiply_convert_fusion.6
  411.5 2.8 constant_dynamic-update-slice_fusion.5
  415.2 3.3 multiply_convert_fusion.5
  419.8 3.9 copy.293
  423.7 3.2 constant_dynamic-update-slice_fusion.4
  427.7 3.2 multiply_convert_fusion.4
  433.9 4.6 copy.294
  438.5 3.5 constant_dynamic-update-slice_fusion.3
  442.8 3.2 multiply_convert_fusion.3
  449.0 4.6 copy.295
  453.6 3.8 constant_dynamic-update-slice_fusion.2
  458.3 3.2 multiply_convert_fusion.2
  464.4 6.0 copy.296
  470.4 3.9 constant_dynamic-update-slice_fusion.1
  475.1 3.2 multiply_convert_fusion.1
  481.3 6.5 copy.297
  487.8 4.2 constant_dynamic-update-slice_fusion
  492.8 3.2 multiply_convert_fusion
  497.3 3.0 copy.282
  513.7 4.0 copy.283
  521.4 2.6 convolution_add_fusion.11
  526.6 5.4 copy.284
  537.7 2.6 convolution_add_fusion.10
  542.8 5.9 copy.285
  552.9 2.6 convolution_add_fusion.9
  558.0 6.7 copy.286
  571.0 2.6 convolution_add_fusion.8
  576.0 8.5 %copy.287 = f32[512,3584]{0,1:T(8,128)} copy(f32[512,3584]{1,0:T(8,128)} %get-tuple-element.232) | data formatting | bytes 14680064 | tf_op jit(solution)/shard_map/div | solution.py:77
  596.4 9.0 %copy.288 = f32[512,4096]{0,1:T(8,128)} copy(f32[512,4096]{1,0:T(8,128)} %get-tuple-element.230) | data formatting | bytes 16777216 | tf_op jit(solution)/shard_map/div | solution.py:77
  605.4 2.6 slice.845
  624.6 17.0 %all-to-all-start.5 = ((f32[32,4,128]{2,1,0:T(4,128)}), f32[32,4,128]{2,1,0:T(4,128)S(1)}, u32[]{:S(2)}, u32[]{:S(2)}) async-start(f32[32,4,128]{2,1,0:T(4,128)} %bitcast.974), calls=%async_computation.5 | async-start | bytes 131072 | tf_op jit(solution)/shard_map/all_to_all | solution.py:132
  653.2 9.8 %all-to-all-start.3 = ((bf16[32,128,128]{2,1,0:T(8,128)(2,1)}), bf16[32,128,128]{2,1,0:T(8,128)(2,1)S(1)}, u32[]{:S(2)}, u32[]{:S(2)}) async-start(bf16[32,128,128]{2,1,0:T(8,128)(2,1)} %bitcast.964), calls=%async_computation.3 | async-start | bytes 2097152 | tf_op jit(solution)/shard_map/all_to_all | solution.py:122
  673.6 18.0 %all-to-all-done.3 = bf16[32,128,128]{2,1,0:T(8,128)(2,1)S(1)} async-done(((bf16[32,128,128]{2,1,0:T(8,128)(2,1)}), bf16[32,128,128]{2,1,0:T(8,128)(2,1)S(1)}, u32[]{:S(2)}, u32[]{:S(2)}) %all-to-all-start.3) | async-done | bytes 1048608 | tf_op jit(solution)/shard_map/all_to_all | solution.py:122
  691.6 5.7 all-to-all-start.7
  699.2 7.8 %all-to-all-done.7 = f32[32,4,128]{2,1,0:T(4,128)S(1)} async-done(((f32[32,4,128]{2,1,0:T(4,128)}), f32[32,4,128]{2,1,0:T(4,128)S(1)}, u32[]{:S(2)}, u32[]{:S(2)}) %all-to-all-start.7) | async-done | bytes 65568 | tf_op jit(solution)/shard_map/all_to_all | solution.py:134
  707.1 3.9 all-to-all-start.6
  712.7 8.1 %all-to-all-done.6 = f32[32,4,128]{2,1,0:T(4,128)S(1)} async-done(((f32[32,4,128]{2,1,0:T(4,128)}), f32[32,4,128]{2,1,0:T(4,128)S(1)}, u32[]{:S(2)}, u32[]{:S(2)}) %all-to-all-start.6) | async-done | bytes 65568 | tf_op jit(solution)/shard_map/all_to_all | solution.py:133
  (602 shorter events, 262.5 us)
Async XLA Ops:
  7.2 14.0 %copy-start.109 = (bf16[128,1024]{1,0:T(8,128)(2,1)S(1)}, bf16[128,1024]{1,0:T(8,128)(2,1)}, u32[]{:S(2)}) copy-start(bf16[128,1024]{1,0:T(8,128)(2,1)} %param.41) | copy-start | bytes 786436
  9.4 40.4 %all-to-all-start.2 = ((bf16[128,32,128]{2,0,1:T(8,128)(2,1)}), bf16[128,32,128]{2,0,1:T(8,128)(2,1)S(1)}, u32[]{:S(2)}, u32[]{:S(2)}) async-start(bf16[128,32,128]{2,0,1:T(8,128)(2,1)} %bitcast.8), calls=%async_computation.2 | async-start | bytes 2097152 | tf_op jit(solution)/shard_map/all_to_all | solution.py:31
  51.0 33.4 %all-to-all-start.1 = ((bf16[128,32,128]{2,0,1:T(8,128)(2,1)}), bf16[128,32,128]{2,0,1:T(8,128)(2,1)S(1)}, u32[]{:S(2)}, u32[]{:S(2)}) async-start(bf16[128,32,128]{2,0,1:T(8,128)(2,1)} %bitcast.867), calls=%async_computation.1 | async-start | bytes 2097152 | tf_op jit(solution)/shard_map/all_to_all | solution.py:30
  84.3 47.3 %all-to-all-start = ((bf16[128,32,128]{0,2,1:T(8,128)(2,1)}), bf16[128,32,128]{0,2,1:T(8,128)(2,1)}, u32[]{:S(2)}, u32[]{:S(2)}) async-start(bf16[128,32,128]{0,2,1:T(8,128)(2,1)} %bitcast.869), calls=%async_computation | async-start | bytes 2097152 | tf_op jit(solution)/shard_map/all_to_all | solution.py:29
  91.9 144.6 %copy-start.156 = (pred[1024]{0:T(1024)(128)(4,1)}, pred[1024]{0:T(1024)(128)(4,1)S(1)}, u32[]{:S(2)}) copy-start(pred[1024]{0:T(1024)(128)(4,1)S(1)} %fusion.338) | copy-start | bytes 3076
  95.7 52.7 %copy-start.106 = (bf16[4,128,128]{2,1,0:T(8,128)(2,1)}, bf16[4,128,128]{2,1,0:T(8,128)(2,1)S(1)}, u32[]{:S(2)}) copy-start(bf16[4,128,128]{2,1,0:T(8,128)(2,1)S(1)} %slice.786) | copy-start | bytes 393220
  131.6 96.7 %all-to-all-start.4 = ((bf16[128,32,128]{0,2,1:T(8,128)(2,1)}), bf16[128,32,128]{0,2,1:T(8,128)(2,1)}, u32[]{:S(2)}, u32[]{:S(2)}) async-start(bf16[128,32,128]{0,2,1:T(8,128)(2,1)} %bitcast.868), calls=%async_computation.4 | async-start | bytes 2097152 | tf_op jit(solution)/shard_map/all_to_all | solution.py:32
  145.9 526.0 %reduce-scatter.2.cloned.1.call-start = ((), (), s32[]{:S(2)}) async-start(), calls=%async_computation.9 | async-start | bytes 1179648 | tf_op jit(solution)/shard_map/reduce_scatter | solution.py:127
  236.5 30.1 %copy-start.32 = (f32[512,1024]{1,0:T(8,128)}, f32[512,1024]{1,0:T(8,128)S(1)}, u32[]{:S(2)}) copy-start(f32[512,1024]{1,0:T(8,128)S(1)} %get-tuple-element.279) | copy-start | bytes 6291460
  243.4 23.3 %copy-start.27 = (f32[512,1024]{1,0:T(8,128)}, f32[512,1024]{1,0:T(8,128)S(1)}, u32[]{:S(2)}) copy-start(f32[512,1024]{1,0:T(8,128)S(1)} %get-tuple-element.277) | copy-start | bytes 6291460
  243.4 23.3 %copy-start.149 = (f32[512]{0:T(512)}, f32[512]{0:T(512)S(1)}, u32[]{:S(2)}) copy-start(f32[512]{0:T(512)S(1)} %max.73) | copy-start | bytes 6148
  244.4 30.2 %copy-start.127 = (f32[512]{0:T(512)}, f32[512]{0:T(512)S(1)}, u32[]{:S(2)}) copy-start(f32[512]{0:T(512)S(1)} %max.74) | copy-start | bytes 6148
  252.4 76.9 %copy-start.118 = (f32[512]{0:T(512)}, f32[512]{0:T(512)S(1)}, u32[]{:S(2)}) copy-start(f32[512]{0:T(512)S(1)} %max.76) | copy-start | bytes 6148
  256.4 77.0 %copy-start.120 = (f32[512]{0:T(512)}, f32[512]{0:T(512)S(1)}, u32[]{:S(2)}) copy-start(f32[512]{0:T(512)S(1)} %max.77) | copy-start | bytes 6148
  260.7 77.1 %copy-start.122 = (f32[512]{0:T(512)}, f32[512]{0:T(512)S(1)}, u32[]{:S(2)}) copy-start(f32[512]{0:T(512)S(1)} %max.78) | copy-start | bytes 6148
  329.3 13.3 %slice-start = ((s8[8388608]{0:T(1024)(128)(4,1)}), s8[4194304]{0:T(1024)(128)(4,1)S(1)}, s32[]{:S(2)}) async-start(s8[8388608]{0:T(1024)(128)(4,1)} %bitcast.820), calls=%async_computation.10 | async-start | bytes 8388608
  333.3 9.3 %slice-start.1 = ((s8[8388608]{0:T(1024)(128)(4,1)}), s8[4194304]{0:T(1024)(128)(4,1)S(1)}, s32[]{:S(2)}) async-start(s8[8388608]{0:T(1024)(128)(4,1)} %bitcast.820), calls=%async_computation.11 | async-start | bytes 8388608
  360.5 8.8 %copy-start.117 = (f32[16,1,128]{2,0,1:T(8,128)}, f32[16,1,128]{2,0,1:T(8,128)S(1)}, u32[]{:S(2)}) copy-start(f32[16,1,128]{2,0,1:T(8,128)S(1)} %fusion.162) | copy-start | bytes 24580
  361.1 8.2 %slice-start.6 = ((s8[6291456]{0:T(1024)(128)(4,1)}), s8[4194304]{0:T(1024)(128)(4,1)S(1)}, s32[]{:S(2)}) async-start(s8[6291456]{0:T(1024)(128)(4,1)} %bitcast.838), calls=%async_computation.16 | async-start | bytes 8388608
  380.9 8.3 %copy-start.28 = (f32[512,1024]{1,0:T(8,128)S(1)}, f32[512,1024]{1,0:T(8,128)}, u32[]{:S(2)}) copy-start(f32[512,1024]{1,0:T(8,128)} %copy-done.27) | copy-start | bytes 6291460
  380.9 8.9 %copy-start.33 = (f32[512,1024]{1,0:T(8,128)S(1)}, f32[512,1024]{1,0:T(8,128)}, u32[]{:S(2)}) copy-start(f32[512,1024]{1,0:T(8,128)} %copy-done.32) | copy-start | bytes 6291460
  380.9 8.9 %copy-start.119 = (f32[512]{0:T(512)S(1)}, f32[512]{0:T(512)}, u32[]{:S(2)}) copy-start(f32[512]{0:T(512)} %copy-done.118) | copy-start | bytes 6148
  380.9 8.9 %copy-start.150 = (f32[512]{0:T(512)S(1)}, f32[512]{0:T(512)}, u32[]{:S(2)}) copy-start(f32[512]{0:T(512)} %copy-done.149) | copy-start | bytes 6148
  380.9 8.9 %copy-start.158 = (pred[1024]{0:T(1024)(128)(4,1)S(1)}, pred[1024]{0:T(1024)(128)(4,1)}, u32[]{:S(2)}) copy-start(pred[1024]{0:T(1024)(128)(4,1)} %copy-done.156) | copy-start | bytes 3076
  500.3 10.6 %copy-start.35 = (bf16[512,1024]{1,0:T(8,128)(2,1)S(1)}, bf16[512,1024]{1,0:T(8,128)(2,1)}, u32[]{:S(2)}) copy-start(bf16[512,1024]{1,0:T(8,128)(2,1)} %multiply_convert_fusion.5) | copy-start | bytes 3145732
  500.3 10.6 %copy-start.71 = (bf16[4,128,128]{2,1,0:T(8,128)(2,1)S(1)}, bf16[4,128,128]{2,1,0:T(8,128)(2,1)}, u32[]{:S(2)}) copy-start(bf16[4,128,128]{2,1,0:T(8,128)(2,1)} %copy.232) | copy-start | bytes 393220
  517.7 8.1 %copy-start.144 = (f32[1,16,32]{2,1,0:T(8,128)S(1)}, f32[1,16,32]{2,1,0:T(8,128)}, u32[]{:S(2)}) copy-start(f32[1,16,32]{2,1,0:T(8,128)} %reshape_transpose.27) | copy-start | bytes 6148
  526.6 11.2 %copy-start.79 = (bf16[4,128,128]{2,1,0:T(8,128)(2,1)S(1)}, bf16[4,128,128]{2,1,0:T(8,128)(2,1)}, u32[]{:S(2)}) copy-start(bf16[4,128,128]{2,1,0:T(8,128)(2,1)} %copy.234) | copy-start | bytes 393220
  532.0 10.1 %copy-start.145 = (f32[1,16,32]{2,1,0:T(8,128)S(1)}, f32[1,16,32]{2,1,0:T(8,128)}, u32[]{:S(2)}) copy-start(f32[1,16,32]{2,1,0:T(8,128)} %reshape_transpose.28) | copy-start | bytes 6148
  542.8 10.1 %copy-start.75 = (bf16[4,128,128]{2,1,0:T(8,128)(2,1)S(1)}, bf16[4,128,128]{2,1,0:T(8,128)(2,1)}, u32[]{:S(2)}) copy-start(bf16[4,128,128]{2,1,0:T(8,128)(2,1)} %copy.235) | copy-start | bytes 393220
  548.7 8.5 %copy-start.146 = (f32[1,16,32]{2,1,0:T(8,128)S(1)}, f32[1,16,32]{2,1,0:T(8,128)}, u32[]{:S(2)}) copy-start(f32[1,16,32]{2,1,0:T(8,128)} %reshape_transpose.29) | copy-start | bytes 6148
  558.0 12.9 %copy-start.67 = (bf16[4,128,128]{2,1,0:T(8,128)(2,1)S(1)}, bf16[4,128,128]{2,1,0:T(8,128)(2,1)}, u32[]{:S(2)}) copy-start(bf16[4,128,128]{2,1,0:T(8,128)(2,1)} %copy.236) | copy-start | bytes 393220
  564.7 10.6 %copy-start.147 = (f32[1,16,32]{2,1,0:T(8,128)S(1)}, f32[1,16,32]{2,1,0:T(8,128)}, u32[]{:S(2)}) copy-start(f32[1,16,32]{2,1,0:T(8,128)} %reshape_transpose.30) | copy-start | bytes 6148
  576.0 14.8 %copy-start.57 = (bf16[4,128,128]{2,1,0:T(8,128)(2,1)S(1)}, bf16[4,128,128]{2,1,0:T(8,128)(2,1)}, u32[]{:S(2)}) copy-start(bf16[4,128,128]{2,1,0:T(8,128)(2,1)} %copy.237) | copy-start | bytes 393220
  605.4 8.7 %copy-start.34 = (bf16[16,128,128]{2,1,0:T(8,128)(2,1)S(1)}, bf16[16,128,128]{2,1,0:T(8,128)(2,1)}, u32[]{:S(2)}) copy-start(bf16[16,128,128]{2,1,0:T(8,128)(2,1)} %slice.797) | copy-start | bytes 1572868
  623.4 28.4 %copy-start.51 = (bf16[4,128,128]{2,1,0:T(8,128)(2,1)S(1)}, bf16[4,128,128]{2,1,0:T(8,128)(2,1)}, u32[]{:S(2)}) copy-start(bf16[4,128,128]{2,1,0:T(8,128)(2,1)} %copy.245) | copy-start | bytes 393220
  623.4 28.4 %copy-start.93 = (f32[128,1,128]{2,0,1:T(8,128)S(1)}, f32[128,1,128]{2,0,1:T(8,128)}, u32[]{:S(2)}) copy-start(f32[128,1,128]{2,0,1:T(8,128)} %scatter-add.59) | copy-start | bytes 196612
  623.5 28.4 %copy-start.114 = (bf16[1,512,32,1]{1,3,2,0:T(2,128)(2,1)S(1)}, bf16[1,512,32,1]{1,3,2,0:T(2,128)(2,1)}, u32[]{:S(2)}) copy-start(bf16[1,512,32,1]{1,3,2,0:T(2,128)(2,1)} %slice.871) | copy-start | bytes 98308
  623.5 28.6 %copy-start.39 = (bf16[4,128,128]{2,1,0:T(8,128)(2,1)S(1)}, bf16[4,128,128]{2,1,0:T(8,128)(2,1)}, u32[]{:S(2)}) copy-start(bf16[4,128,128]{2,1,0:T(8,128)(2,1)} %copy.250) | copy-start | bytes 393220
  623.5 28.6 %copy-start.112 = (bf16[1,512,48,1]{1,3,2,0:T(2,128)(2,1)S(1)}, bf16[1,512,48,1]{1,3,2,0:T(2,128)(2,1)}, u32[]{:S(2)}) copy-start(bf16[1,512,48,1]{1,3,2,0:T(2,128)(2,1)} %slice.873) | copy-start | bytes 147460
  624.6 27.6 %copy-start.49 = (bf16[4,128,128]{2,1,0:T(8,128)(2,1)S(1)}, bf16[4,128,128]{2,1,0:T(8,128)(2,1)}, u32[]{:S(2)}) copy-start(bf16[4,128,128]{2,1,0:T(8,128)(2,1)} %copy.255) | copy-start | bytes 393220
  624.6 27.6 %copy-start.108 = (bf16[1,512,64,1]{1,3,2,0:T(2,128)(2,1)S(1)}, bf16[1,512,64,1]{1,3,2,0:T(2,128)(2,1)}, u32[]{:S(2)}) copy-start(bf16[1,512,64,1]{1,3,2,0:T(2,128)(2,1)} %slice.875) | copy-start | bytes 196612
  624.6 27.8 %copy-start.47 = (bf16[4,128,128]{2,1,0:T(8,128)(2,1)S(1)}, bf16[4,128,128]{2,1,0:T(8,128)(2,1)}, u32[]{:S(2)}) copy-start(bf16[4,128,128]{2,1,0:T(8,128)(2,1)} %copy.260) | copy-start | bytes 393220
  624.6 27.8 %copy-start.107 = (bf16[1,512,80,1]{1,3,2,0:T(2,128)(2,1)S(1)}, bf16[1,512,80,1]{1,3,2,0:T(2,128)(2,1)}, u32[]{:S(2)}) copy-start(bf16[1,512,80,1]{1,3,2,0:T(2,128)(2,1)} %slice.877) | copy-start | bytes 245764
  624.6 28.0 %all-to-all-start.5 = ((f32[32,4,128]{2,1,0:T(4,128)}), f32[32,4,128]{2,1,0:T(4,128)S(1)}, u32[]{:S(2)}, u32[]{:S(2)}) async-start(f32[32,4,128]{2,1,0:T(4,128)} %bitcast.974), calls=%async_computation.5 | async-start | bytes 131072 | tf_op jit(solution)/shard_map/all_to_all | solution.py:132
  649.8 13.3 %copy-start.45 = (bf16[4,128,128]{2,1,0:T(8,128)(2,1)S(1)}, bf16[4,128,128]{2,1,0:T(8,128)(2,1)}, u32[]{:S(2)}) copy-start(bf16[4,128,128]{2,1,0:T(8,128)(2,1)} %copy.265) | copy-start | bytes 393220
  649.8 14.4 %copy-start.87 = (bf16[4,128,128]{2,1,0:T(8,128)(2,1)S(1)}, bf16[4,128,128]{2,1,0:T(8,128)(2,1)}, u32[]{:S(2)}) copy-start(bf16[4,128,128]{2,1,0:T(8,128)(2,1)} %copy.231) | copy-start | bytes 393220
  649.8 14.4 %copy-start.92 = (f32[128,1,128]{2,0,1:T(8,128)S(1)}, f32[128,1,128]{2,0,1:T(8,128)}, u32[]{:S(2)}) copy-start(f32[128,1,128]{2,0,1:T(8,128)} %scatter-add.46) | copy-start | bytes 196612
  651.7 13.6 %copy-start.43 = (bf16[4,128,128]{2,1,0:T(8,128)(2,1)S(1)}, bf16[4,128,128]{2,1,0:T(8,128)(2,1)}, u32[]{:S(2)}) copy-start(bf16[4,128,128]{2,1,0:T(8,128)(2,1)} %copy.270) | copy-start | bytes 393220
  651.9 14.7 %copy-start.72 = (bf16[4,128,128]{2,1,0:T(8,128)(2,1)S(1)}, bf16[4,128,128]{2,1,0:T(8,128)(2,1)}, u32[]{:S(2)}) copy-start(bf16[4,128,128]{2,1,0:T(8,128)(2,1)} %copy.232) | copy-start | bytes 393220
  652.2 15.5 %copy-start.84 = (bf16[4,128,128]{2,1,0:T(8,128)(2,1)S(1)}, bf16[4,128,128]{2,1,0:T(8,128)(2,1)}, u32[]{:S(2)}) copy-start(bf16[4,128,128]{2,1,0:T(8,128)(2,1)} %copy.233) | copy-start | bytes 393220
  652.6 16.4 %copy-start.80 = (bf16[4,128,128]{2,1,0:T(8,128)(2,1)S(1)}, bf16[4,128,128]{2,1,0:T(8,128)(2,1)}, u32[]{:S(2)}) copy-start(bf16[4,128,128]{2,1,0:T(8,128)(2,1)} %copy.234) | copy-start | bytes 393220
  652.6 17.6 %copy-start.76 = (bf16[4,128,128]{2,1,0:T(8,128)(2,1)S(1)}, bf16[4,128,128]{2,1,0:T(8,128)(2,1)}, u32[]{:S(2)}) copy-start(bf16[4,128,128]{2,1,0:T(8,128)(2,1)} %copy.235) | copy-start | bytes 393220
  652.6 17.6 %copy-start.116 = (bf16[96,1,1,128]{3,1,0,2:T(2,128)(2,1)S(1)}, bf16[96,1,1,128]{3,1,0,2:T(2,128)(2,1)}, u32[]{:S(2)}) copy-start(bf16[96,1,1,128]{3,1,0,2:T(2,128)(2,1)} %slice.863) | copy-start | bytes 73732
  652.6 18.9 %copy-start.68 = (bf16[4,128,128]{2,1,0:T(8,128)(2,1)S(1)}, bf16[4,128,128]{2,1,0:T(8,128)(2,1)}, u32[]{:S(2)}) copy-start(bf16[4,128,128]{2,1,0:T(8,128)(2,1)} %copy.236) | copy-start | bytes 393220
  653.2 38.4 %all-to-all-start.3 = ((bf16[32,128,128]{2,1,0:T(8,128)(2,1)}), bf16[32,128,128]{2,1,0:T(8,128)(2,1)S(1)}, u32[]{:S(2)}, u32[]{:S(2)}) async-start(bf16[32,128,128]{2,1,0:T(8,128)(2,1)} %bitcast.964), calls=%async_computation.3 | async-start | bytes 2097152 | tf_op jit(solution)/shard_map/all_to_all | solution.py:122
  663.1 8.8 %copy-start.41 = (bf16[4,128,128]{2,1,0:T(8,128)(2,1)S(1)}, bf16[4,128,128]{2,1,0:T(8,128)(2,1)}, u32[]{:S(2)}) copy-start(bf16[4,128,128]{2,1,0:T(8,128)(2,1)} %copy.275) | copy-start | bytes 393220
  663.1 34.3 %copy-start.58 = (bf16[4,128,128]{2,1,0:T(8,128)(2,1)S(1)}, bf16[4,128,128]{2,1,0:T(8,128)(2,1)}, u32[]{:S(2)}) copy-start(bf16[4,128,128]{2,1,0:T(8,128)(2,1)} %copy.237) | copy-start | bytes 393220
  665.4 31.9 %copy-start.113 = (bf16[128,1,1,128]{3,1,0,2:T(2,128)(2,1)S(1)}, bf16[128,1,1,128]{3,1,0,2:T(2,128)(2,1)}, u32[]{:S(2)}) copy-start(bf16[128,1,1,128]{3,1,0,2:T(2,128)(2,1)} %slice.868) | copy-start | bytes 98308
  665.4 31.9 %copy-start.134 = (f32[512]{0:T(512)S(1)}, f32[512]{0:T(512)}, u32[]{:S(2)}) copy-start(f32[512]{0:T(512)} %copy-done.133) | copy-start | bytes 6148
  671.5 49.9 %copy-start.111 = (f32[32,4,128]{2,1,0:T(4,128)S(1)}, f32[32,4,128]{2,1,0:T(4,128)}, u32[]{:S(2)}) copy-start(f32[32,4,128]{2,1,0:T(4,128)} %copy-done.110) | copy-start | bytes 196612
  671.5 50.5 %copy-start.1 = (bf16[128,1024]{1,0:T(8,128)(2,1)S(1)}, bf16[128,1024]{1,0:T(8,128)(2,1)}, u32[]{:S(2)}) copy-start(bf16[128,1024]{1,0:T(8,128)(2,1)} %param.42) | copy-start | bytes 786436
  691.6 15.5 %all-to-all-start.7 = ((f32[32,4,128]{2,1,0:T(4,128)}), f32[32,4,128]{2,1,0:T(4,128)S(1)}, u32[]{:S(2)}, u32[]{:S(2)}) async-start(f32[32,4,128]{2,1,0:T(4,128)} %bitcast.242), calls=%async_computation.8 | async-start | bytes 131072 | tf_op jit(solution)/shard_map/all_to_all | solution.py:134
  707.1 13.8 %all-to-all-start.6 = ((f32[32,4,128]{2,1,0:T(4,128)}), f32[32,4,128]{2,1,0:T(4,128)S(1)}, u32[]{:S(2)}, u32[]{:S(2)}) async-start(f32[32,4,128]{2,1,0:T(4,128)} %bitcast.204), calls=%async_computation.7 | async-start | bytes 131072 | tf_op jit(solution)/shard_map/all_to_all | solution.py:133
  (128 other events, 550.5 us)
Sparse Core Ops, SparseCore 0:
  595.7 43.3 reduce-scatter.1
where the time goes:
time: 741 us; the launch traced here: 729 us
  local copies, waits for them, and re-layouts  236 us (32%)
  matrix products  165 us (22%)
  waiting for transfers between devices  88.7 us (12%)
  other arithmetic  77.3 us (10%)
  blocking collectives  73.2 us (10%)
  starting transfers between devices  72.7 us (10%)
  between operations  16.1 us (2%)
    div x8, local copies, waits for them, and re-layouts, on_device(): p_local = e_local / denom[:, :, None]  45.1 us
    convert_element_type x8, other arithmetic, on_device(): b_local = p_local.astype(jnp.bfloat16)  40.5 us
    all_gather x1, blocking collectives, on_device(): lax.all_gather(own_k, 'span', axis=0, tiled=True)  37.2 us
    all_gather x1, blocking collectives, on_device(): lax.all_gather(own_v, 'span', axis=0, tiled=True)  35.9 us
    convert_element_type x7, local copies, waits for them, and re-layouts, on_device(): b_local = p_local.astype(jnp.bfloat16)  30.5 us
    all_to_all x1, waiting for transfers between devices, on_device(): lax.all_to_all(widen(value), 'ulysses', split_axis=1, concat_axis=0, tile...  28.5 us
    all_to_all x1, waiting for transfers between devices, on_device(): lax.all_to_all(widen(key), 'ulysses', split_axis=1, concat_axis=0, tiled=...  26.2 us
    dot_general x8, matrix products, on_device(): jnp.einsum('hqk,khd->qhd', b_local, v_loc, preferred_element_type=jnp.flo...  24.8 us
  transfers between devices with their start and end apart: 9, of which 5 were waited for; matrix products, arithmetic and copies ran while one was open for 15% of the time, Pallas kernels for 0%

commit v1 on v0

--- a/solution.py
+++ b/solution.py
@@ -34,7 +34,9 @@
     own_k = k_h.reshape(beacons, INTERVAL, per_dev * HD)[:, -1]
     own_v = v_h.reshape(beacons, INTERVAL, per_dev * HD)[:, -1]
     prior_k, prior_v = (
-        lax.all_gather(own_k, "span", axis=0, tiled=True),
+        jnp.concatenate(
+            lax.all_to_all(jnp.stack([own_k] * lax.axis_size("span")), "span", 0, 0), axis=0
+        ),
         lax.all_gather(own_v, "span", axis=0, tiled=True),
     )
     all_beacons = prior_k.shape[0]

time: 741 us -> 699 us (0.943)
  blocking collectives: 73.2 us -> 24 us
  waiting for transfers between devices: 88.7 us -> 108 us
    all_gather x1 -> x0, blocking collectives: 37.2 us -> none  [on_device(): lax.all_gather(own_k, 'span', axis=0, tiled=True)]
    all_to_all x1, waiting for transfers between devices: 0.01 us -> 23.2 us  [on_device(): lax.all_to_all(query, 'ulysses', split_axis=1, concat_axis=0, tiled=True)]
    dot_general x8, matrix products: 20.3 us -> 7.03 us  [on_device(): jnp.einsum('qhd,khd->hqk', q_blk, pk3, preferred_element_type=jnp.float32)]
    all_gather x1, blocking collectives: 35.9 us -> 24 us  [on_device(): lax.all_gather(own_v, 'span', axis=0, tiled=True)]
    dot_general x8, matrix products: 22.1 us -> 30.8 us  [on_device(): jnp.einsum('qhd,khd->hqk', q_blk, k_loc, preferred_element_type=jnp.float32)]
    unnamed x369 -> x376, local copies, waits for them, and re-layouts: 20 us -> 18.2 us
  transfers between devices with their start and end apart: 9 -> 10, of which waited for: 5 -> 6; matrix products, arithmetic and copies ran while one was open for 15% -> 23% of each run, Pallas kernels for 0% -> 0%
where the time goes in v1:
time: 699 us; the launch traced here: 689 us
  local copies, waits for them, and re-layouts  234 us (33%)
  matrix products  160 us (23%)
  waiting for transfers between devices  108 us (15%)
  starting transfers between devices  74 us (11%)
  other arithmetic  71.9 us (10%)
  blocking collectives  24 us (3%)
  between operations  16.2 us (2%)
    div x8, local copies, waits for them, and re-layouts, on_device(): p_local = e_local / denom[:, :, None]  44.8 us
    convert_element_type x8, other arithmetic, on_device(): b_local = p_local.astype(jnp.bfloat16)  42.7 us
    dot_general x8, matrix products, on_device(): jnp.einsum('qhd,khd->hqk', q_blk, k_loc, preferred_element_type=jnp.float32)  30.8 us
    convert_element_type x7, local copies, waits for them, and re-layouts, on_device(): b_local = p_local.astype(jnp.bfloat16)  30.4 us
    all_to_all x1, waiting for transfers between devices, on_device(): lax.all_to_all(widen(value), 'ulysses', split_axis=1, concat_axis=0, tile...  28.5 us
    all_to_all x1, waiting for transfers between devices, on_device(): lax.all_to_all(widen(key), 'ulysses', split_axis=1, concat_axis=0, tiled=...  26.2 us
    dot_general x8, matrix products, on_device(): jnp.einsum('hqk,khd->qhd', b_local, v_loc, preferred_element_type=jnp.flo...  24.7 us
    dot_general x8, matrix products, on_device(): jnp.einsum('qhd,khd->hqk', g_blk, pv3, preferred_element_type=jnp.float32)  24.1 us
  transfers between devices with their start and end apart: 10, of which 6 were waited for; matrix products, arithmetic and copies ran while one was open for 23% of the time, Pallas kernels for 0%

profile of v1, /device:TPU:9, one launch (start us, length us, event | category | flops | bytes accessed | tf_op | source)
XLA Modules:
  0.0 688.8 jit_solution(9515768144443243157)
XLA Ops:
  9.4 11.8 %all-to-all-start.3 = ((bf16[128,32,128]{2,0,1:T(8,128)(2,1)}), bf16[128,32,128]{2,0,1:T(8,128)(2,1)S(1)}, u32[]{:S(2)}, u32[]{:S(2)}) async-start(bf16[128,32,128]{2,0,1:T(8,128)(2,1)} %bitcast.8), calls=%async_computation.3 | async-start | bytes 2097152 | tf_op jit(solution)/shard_map/all_to_all | solution.py:31
  21.2 28.5 %all-to-all-done.3 = bf16[128,32,128]{2,0,1:T(8,128)(2,1)S(1)} async-done(((bf16[128,32,128]{2,0,1:T(8,128)(2,1)}), bf16[128,32,128]{2,0,1:T(8,128)(2,1)S(1)}, u32[]{:S(2)}, u32[]{:S(2)}) %all-to-all-start.3) | async-done | bytes 1048608 | tf_op jit(solution)/shard_map/all_to_all | solution.py:31
  51.0 4.9 all-to-all-start.1
  58.2 26.2 %all-to-all-done.1 = bf16[128,32,128]{2,0,1:T(8,128)(2,1)S(1)} async-done(((bf16[128,32,128]{2,0,1:T(8,128)(2,1)}), bf16[128,32,128]{2,0,1:T(8,128)(2,1)S(1)}, u32[]{:S(2)}, u32[]{:S(2)}) %all-to-all-start.1) | async-done | bytes 1048608 | tf_op jit(solution)/shard_map/all_to_all | solution.py:30
  84.3 5.3 all-to-all-start
  91.9 23.2 %all-to-all-done = bf16[128,32,128]{0,2,1:T(8,128)(2,1)} async-done(((bf16[128,32,128]{0,2,1:T(8,128)(2,1)}), bf16[128,32,128]{0,2,1:T(8,128)(2,1)}, u32[]{:S(2)}, u32[]{:S(2)}) %all-to-all-start) | async-done | bytes 1048608 | tf_op jit(solution)/shard_map/all_to_all | solution.py:29
  115.1 8.1 %all-to-all-start.5 = ((bf16[128,32,128]{0,2,1:T(8,128)(2,1)}), bf16[128,32,128]{0,2,1:T(8,128)(2,1)}, u32[]{:S(2)}, u32[]{:S(2)}) async-start(bf16[128,32,128]{0,2,1:T(8,128)(2,1)} %bitcast.873), calls=%async_computation.5 | async-start | bytes 2097152 | tf_op jit(solution)/shard_map/all_to_all | solution.py:32
  154.8 24.0 %all-gather = bf16[1024,1,128]{2,0,1:T(8,128)(2,1)S(1)} all-gather(bf16[128,1,128]{2,0,1:T(8,128)(2,1)} %copy.229), channel_id=2, replica_groups=mesh['span'=8,'ulysses'=32] {'span'}, dimensions={0}, use_global_device_ids=true | all-gather | bytes 294912 | tf_op jit(solution)/shard_map/all_gather | solution.py:40
  180.3 4.6 all-to-all-start.2
  185.3 3.0 slice_convert_fusion
  226.7 2.8 fusion.378
  229.5 3.4 fusion.371
  235.3 3.5 fusion.376
  238.9 3.9 fusion.375
  242.8 4.4 fusion.374
  247.2 4.9 fusion.373
  252.1 5.5 fusion.372
  262.1 2.9 fusion.34
  269.7 5.1 fusion.28
  275.9 2.8 fusion.41
  285.4 5.1 fusion.364
  290.5 5.8 fusion.362
  296.3 4.1 fusion.7
  322.9 7.3 %fusion.360 = (bf16[512,2560]{1,0:T(8,128)(2,1)}, f32[512,2560]{1,0:T(8,128)}) fusion(f32[512]{0:T(512)S(1)} %add.460, f32[512,2560]{1,0:T(8,128)} %get-tuple-element.287, f32[512]{0:T(512)} %copy-done.113), kind=kLoop, calls=%fused_computation.488 | loop fusion | flops 3932160 | bytes 13111296 | tf_op jit(solution)/shard_map/convert_element_type | solution.py:81
  330.3 5.3 fusion.358
  336.4 5.4 fusion.356
  341.9 7.2 %fusion.354 = (bf16[512,4096]{1,0:T(8,128)(2,1)}, f32[512,4096]{1,0:T(8,128)}) fusion(f32[512]{0:T(512)S(1)} %add.472, f32[512,4096]{1,0:T(8,128)S(1)} %bitcast.824, f32[512]{0:T(512)S(1)} %copy-done.121), kind=kLoop, calls=%fused_computation.485 | loop fusion | flops 6291456 | bytes 20975616 | tf_op jit(solution)/shard_map/convert_element_type | solution.py:81
  350.8 5.6 fusion.366
  365.4 3.2 multiply_convert_fusion.6
  372.5 2.8 constant_dynamic-update-slice_fusion.5
  376.1 3.3 multiply_convert_fusion.5
  380.7 3.9 copy.292
  384.6 3.2 constant_dynamic-update-slice_fusion.4
  388.6 3.3 multiply_convert_fusion.4
  394.9 4.4 copy.293
  399.3 3.5 constant_dynamic-update-slice_fusion.3
  403.6 3.2 multiply_convert_fusion.3
  409.8 4.8 copy.294
  414.6 3.8 constant_dynamic-update-slice_fusion.2
  419.3 3.2 multiply_convert_fusion.2
  425.4 5.9 copy.295
  431.4 3.9 constant_dynamic-update-slice_fusion.1
  436.1 3.2 multiply_convert_fusion.1
  442.2 6.5 copy.296
  448.7 4.2 constant_dynamic-update-slice_fusion
  453.7 3.2 multiply_convert_fusion
  458.2 3.0 copy.281
  474.6 3.6 copy.282
  481.9 2.6 convolution_add_fusion.11
  487.0 5.7 copy.283
  498.3 2.6 convolution_add_fusion.10
  503.4 5.9 copy.284
  518.6 6.6 copy.285
  531.5 2.6 convolution_add_fusion.8
  536.6 8.5 %copy.286 = f32[512,3584]{0,1:T(8,128)} copy(f32[512,3584]{1,0:T(8,128)} %get-tuple-element.232) | data formatting | bytes 14680064 | tf_op jit(solution)/shard_map/div | solution.py:79
  556.9 9.0 %copy.287 = f32[512,4096]{0,1:T(8,128)} copy(f32[512,4096]{1,0:T(8,128)} %get-tuple-element.230) | data formatting | bytes 16777216 | tf_op jit(solution)/shard_map/div | solution.py:79
  566.0 2.6 slice.845
  585.2 17.0 %all-to-all-start.6 = ((f32[32,4,128]{2,1,0:T(4,128)}), f32[32,4,128]{2,1,0:T(4,128)S(1)}, u32[]{:S(2)}, u32[]{:S(2)}) async-start(f32[32,4,128]{2,1,0:T(4,128)} %bitcast.980), calls=%async_computation.6 | async-start | bytes 131072 | tf_op jit(solution)/shard_map/all_to_all | solution.py:134
  613.8 9.8 %all-to-all-start.4 = ((bf16[32,128,128]{2,1,0:T(8,128)(2,1)}), bf16[32,128,128]{2,1,0:T(8,128)(2,1)S(1)}, u32[]{:S(2)}, u32[]{:S(2)}) async-start(bf16[32,128,128]{2,1,0:T(8,128)(2,1)} %bitcast.969), calls=%async_computation.4 | async-start | bytes 2097152 | tf_op jit(solution)/shard_map/all_to_all | solution.py:124
  634.2 14.4 %all-to-all-done.4 = bf16[32,128,128]{2,1,0:T(8,128)(2,1)S(1)} async-done(((bf16[32,128,128]{2,1,0:T(8,128)(2,1)}), bf16[32,128,128]{2,1,0:T(8,128)(2,1)S(1)}, u32[]{:S(2)}, u32[]{:S(2)}) %all-to-all-start.4) | async-done | bytes 1048608 | tf_op jit(solution)/shard_map/all_to_all | solution.py:124
  648.6 8.3 %all-to-all-start.8 = ((f32[32,4,128]{2,1,0:T(4,128)}), f32[32,4,128]{2,1,0:T(4,128)S(1)}, u32[]{:S(2)}, u32[]{:S(2)}) async-start(f32[32,4,128]{2,1,0:T(4,128)} %bitcast.242), calls=%async_computation.9 | async-start | bytes 131072 | tf_op jit(solution)/shard_map/all_to_all | solution.py:136
  658.8 7.8 %all-to-all-done.8 = f32[32,4,128]{2,1,0:T(4,128)S(1)} async-done(((f32[32,4,128]{2,1,0:T(4,128)}), f32[32,4,128]{2,1,0:T(4,128)S(1)}, u32[]{:S(2)}, u32[]{:S(2)}) %all-to-all-start.8) | async-done | bytes 65568 | tf_op jit(solution)/shard_map/all_to_all | solution.py:136
  666.7 3.9 all-to-all-start.7
  672.3 8.1 %all-to-all-done.7 = f32[32,4,128]{2,1,0:T(4,128)S(1)} async-done(((f32[32,4,128]{2,1,0:T(4,128)}), f32[32,4,128]{2,1,0:T(4,128)S(1)}, u32[]{:S(2)}, u32[]{:S(2)}) %all-to-all-start.7) | async-done | bytes 65568 | tf_op jit(solution)/shard_map/all_to_all | solution.py:135
  (612 shorter events, 256.7 us)
Async XLA Ops:
  7.2 14.0 %copy-start.104 = (bf16[128,1024]{1,0:T(8,128)(2,1)S(1)}, bf16[128,1024]{1,0:T(8,128)(2,1)}, u32[]{:S(2)}) copy-start(bf16[128,1024]{1,0:T(8,128)(2,1)} %param.41) | copy-start | bytes 786436
  9.4 40.4 %all-to-all-start.3 = ((bf16[128,32,128]{2,0,1:T(8,128)(2,1)}), bf16[128,32,128]{2,0,1:T(8,128)(2,1)S(1)}, u32[]{:S(2)}, u32[]{:S(2)}) async-start(bf16[128,32,128]{2,0,1:T(8,128)(2,1)} %bitcast.8), calls=%async_computation.3 | async-start | bytes 2097152 | tf_op jit(solution)/shard_map/all_to_all | solution.py:31
  51.0 33.4 %all-to-all-start.1 = ((bf16[128,32,128]{2,0,1:T(8,128)(2,1)}), bf16[128,32,128]{2,0,1:T(8,128)(2,1)S(1)}, u32[]{:S(2)}, u32[]{:S(2)}) async-start(bf16[128,32,128]{2,0,1:T(8,128)(2,1)} %bitcast.872), calls=%async_computation.1 | async-start | bytes 2097152 | tf_op jit(solution)/shard_map/all_to_all | solution.py:30
  84.3 30.7 %all-to-all-start = ((bf16[128,32,128]{0,2,1:T(8,128)(2,1)}), bf16[128,32,128]{0,2,1:T(8,128)(2,1)}, u32[]{:S(2)}, u32[]{:S(2)}) async-start(bf16[128,32,128]{0,2,1:T(8,128)(2,1)} %bitcast.874), calls=%async_computation | async-start | bytes 2097152 | tf_op jit(solution)/shard_map/all_to_all | solution.py:29
  115.1 63.7 %all-to-all-start.5 = ((bf16[128,32,128]{0,2,1:T(8,128)(2,1)}), bf16[128,32,128]{0,2,1:T(8,128)(2,1)}, u32[]{:S(2)}, u32[]{:S(2)}) async-start(bf16[128,32,128]{0,2,1:T(8,128)(2,1)} %bitcast.873), calls=%async_computation.5 | async-start | bytes 2097152 | tf_op jit(solution)/shard_map/all_to_all | solution.py:32
  123.2 138.9 %copy-start.150 = (pred[1024]{0:T(1024)(128)(4,1)}, pred[1024]{0:T(1024)(128)(4,1)S(1)}, u32[]{:S(2)}) copy-start(pred[1024]{0:T(1024)(128)(4,1)S(1)} %fusion.314) | copy-start | bytes 3076
  180.3 77.3 %all-to-all-start.2 = ((bf16[8,128,128]{2,1,0:T(8,128)(2,1)}), bf16[8,128,128]{2,1,0:T(8,128)(2,1)S(1)}, u32[]{:S(2)}, u32[]{:S(2)}) async-start(bf16[8,128,128]{2,1,0:T(8,128)(2,1)} %stack.6), calls=%async_computation.2 | async-start | bytes 524288 | tf_op jit(solution)/shard_map/all_to_all | solution.py:38
  184.9 447.6 %reduce-scatter.2.cloned.1.call-start = ((), (), s32[]{:S(2)}) async-start(), calls=%async_computation.10 | async-start | bytes 1179648 | tf_op jit(solution)/shard_map/reduce_scatter | solution.py:129
  259.5 9.5 %copy-start.2 = (f32[512,1024]{1,0:T(8,128)}, f32[512,1024]{1,0:T(8,128)S(1)}, u32[]{:S(2)}) copy-start(f32[512,1024]{1,0:T(8,128)S(1)} %fusion.380) | copy-start | bytes 6291460
  265.3 10.6 %copy-start.122 = (f32[512]{0:T(512)}, f32[512]{0:T(512)S(1)}, u32[]{:S(2)}) copy-start(f32[512]{0:T(512)S(1)} %max.74) | copy-start | bytes 6148
  268.8 27.5 %copy-start.113 = (f32[512]{0:T(512)}, f32[512]{0:T(512)S(1)}, u32[]{:S(2)}) copy-start(f32[512]{0:T(512)S(1)} %max.76) | copy-start | bytes 6148
  268.8 31.5 %copy-start.115 = (f32[512]{0:T(512)}, f32[512]{0:T(512)S(1)}, u32[]{:S(2)}) copy-start(f32[512]{0:T(512)S(1)} %max.77) | copy-start | bytes 6148
  268.9 33.1 %copy-start.117 = (f32[512]{0:T(512)}, f32[512]{0:T(512)S(1)}, u32[]{:S(2)}) copy-start(f32[512]{0:T(512)S(1)} %max.78) | copy-start | bytes 6148
  285.4 14.9 %slice-start.8 = ((s8[6291456]{0:T(1024)(128)(4,1)}), s8[4194304]{0:T(1024)(128)(4,1)S(1)}, s32[]{:S(2)}) async-start(s8[6291456]{0:T(1024)(128)(4,1)} %bitcast.841), calls=%async_computation.19 | async-start | bytes 8388608
  285.4 16.5 %slice-start.4 = ((s8[7340032]{0:T(1024)(128)(4,1)}), s8[4194304]{0:T(1024)(128)(4,1)S(1)}, s32[]{:S(2)}) async-start(s8[7340032]{0:T(1024)(128)(4,1)} %bitcast.836), calls=%async_computation.15 | async-start | bytes 8388608
  290.5 9.9 %slice-start.9 = ((s8[6291456]{0:T(1024)(128)(4,1)}), s8[2097152]{0:T(1024)(128)(4,1)S(1)}, s32[]{:S(2)}) async-start(s8[6291456]{0:T(1024)(128)(4,1)} %bitcast.841), calls=%async_computation.20 | async-start | bytes 4194304
  290.5 11.5 %slice-start.5 = ((s8[7340032]{0:T(1024)(128)(4,1)}), s8[3145728]{0:T(1024)(128)(4,1)S(1)}, s32[]{:S(2)}) async-start(s8[7340032]{0:T(1024)(128)(4,1)} %bitcast.836), calls=%async_computation.16 | async-start | bytes 6291456
  321.5 8.8 %copy-start.112 = (f32[16,1,128]{2,0,1:T(8,128)}, f32[16,1,128]{2,0,1:T(8,128)S(1)}, u32[]{:S(2)}) copy-start(f32[16,1,128]{2,0,1:T(8,128)S(1)} %fusion.162) | copy-start | bytes 24580
  322.1 8.2 %slice-start.10 = ((s8[6291456]{0:T(1024)(128)(4,1)}), s8[4194304]{0:T(1024)(128)(4,1)S(1)}, s32[]{:S(2)}) async-start(s8[6291456]{0:T(1024)(128)(4,1)} %bitcast.843), calls=%async_computation.21 | async-start | bytes 8388608
  341.9 8.3 %copy-start.25 = (f32[512,1024]{1,0:T(8,128)S(1)}, f32[512,1024]{1,0:T(8,128)}, u32[]{:S(2)}) copy-start(f32[512,1024]{1,0:T(8,128)} %copy-done.24) | copy-start | bytes 6291460
  341.9 8.9 %copy-start.29 = (f32[512,1024]{1,0:T(8,128)S(1)}, f32[512,1024]{1,0:T(8,128)}, u32[]{:S(2)}) copy-start(f32[512,1024]{1,0:T(8,128)} %get-tuple-element.279) | copy-start | bytes 6291460
  341.9 8.9 %copy-start.114 = (f32[512]{0:T(512)S(1)}, f32[512]{0:T(512)}, u32[]{:S(2)}) copy-start(f32[512]{0:T(512)} %copy-done.113) | copy-start | bytes 6148
  341.9 8.9 %copy-start.145 = (f32[512]{0:T(512)S(1)}, f32[512]{0:T(512)}, u32[]{:S(2)}) copy-start(f32[512]{0:T(512)} %copy-done.144) | copy-start | bytes 6148
  341.9 8.9 %copy-start.152 = (pred[1024]{0:T(1024)(128)(4,1)S(1)}, pred[1024]{0:T(1024)(128)(4,1)}, u32[]{:S(2)}) copy-start(pred[1024]{0:T(1024)(128)(4,1)} %copy-done.150) | copy-start | bytes 3076
  461.2 10.5 %copy-start.31 = (bf16[512,1024]{1,0:T(8,128)(2,1)S(1)}, bf16[512,1024]{1,0:T(8,128)(2,1)}, u32[]{:S(2)}) copy-start(bf16[512,1024]{1,0:T(8,128)(2,1)} %multiply_convert_fusion.5) | copy-start | bytes 3145732
  461.2 10.5 %copy-start.68 = (bf16[4,128,128]{2,1,0:T(8,128)(2,1)S(1)}, bf16[4,128,128]{2,1,0:T(8,128)(2,1)}, u32[]{:S(2)}) copy-start(bf16[4,128,128]{2,1,0:T(8,128)(2,1)} %copy.231) | copy-start | bytes 393220
  478.1 8.1 %copy-start.139 = (f32[1,16,32]{2,1,0:T(8,128)S(1)}, f32[1,16,32]{2,1,0:T(8,128)}, u32[]{:S(2)}) copy-start(f32[1,16,32]{2,1,0:T(8,128)} %reshape_transpose.27) | copy-start | bytes 6148
  487.0 11.3 %copy-start.76 = (bf16[4,128,128]{2,1,0:T(8,128)(2,1)S(1)}, bf16[4,128,128]{2,1,0:T(8,128)(2,1)}, u32[]{:S(2)}) copy-start(bf16[4,128,128]{2,1,0:T(8,128)(2,1)} %copy.233) | copy-start | bytes 393220
  492.6 10.0 %copy-start.140 = (f32[1,16,32]{2,1,0:T(8,128)S(1)}, f32[1,16,32]{2,1,0:T(8,128)}, u32[]{:S(2)}) copy-start(f32[1,16,32]{2,1,0:T(8,128)} %reshape_transpose.28) | copy-start | bytes 6148
  503.4 10.1 %copy-start.72 = (bf16[4,128,128]{2,1,0:T(8,128)(2,1)S(1)}, bf16[4,128,128]{2,1,0:T(8,128)(2,1)}, u32[]{:S(2)}) copy-start(bf16[4,128,128]{2,1,0:T(8,128)(2,1)} %copy.234) | copy-start | bytes 393220
  509.3 8.5 %copy-start.141 = (f32[1,16,32]{2,1,0:T(8,128)S(1)}, f32[1,16,32]{2,1,0:T(8,128)}, u32[]{:S(2)}) copy-start(f32[1,16,32]{2,1,0:T(8,128)} %reshape_transpose.29) | copy-start | bytes 6148
  518.6 12.9 %copy-start.64 = (bf16[4,128,128]{2,1,0:T(8,128)(2,1)S(1)}, bf16[4,128,128]{2,1,0:T(8,128)(2,1)}, u32[]{:S(2)}) copy-start(bf16[4,128,128]{2,1,0:T(8,128)(2,1)} %copy.235) | copy-start | bytes 393220
  525.2 10.6 %copy-start.142 = (f32[1,16,32]{2,1,0:T(8,128)S(1)}, f32[1,16,32]{2,1,0:T(8,128)}, u32[]{:S(2)}) copy-start(f32[1,16,32]{2,1,0:T(8,128)} %reshape_transpose.30) | copy-start | bytes 6148
  536.6 14.8 %copy-start.54 = (bf16[4,128,128]{2,1,0:T(8,128)(2,1)S(1)}, bf16[4,128,128]{2,1,0:T(8,128)(2,1)}, u32[]{:S(2)}) copy-start(bf16[4,128,128]{2,1,0:T(8,128)(2,1)} %copy.236) | copy-start | bytes 393220
  566.0 8.7 %copy-start.30 = (bf16[16,128,128]{2,1,0:T(8,128)(2,1)S(1)}, bf16[16,128,128]{2,1,0:T(8,128)(2,1)}, u32[]{:S(2)}) copy-start(bf16[16,128,128]{2,1,0:T(8,128)(2,1)} %slice.797) | copy-start | bytes 1572868
  584.0 28.5 %copy-start.47 = (bf16[4,128,128]{2,1,0:T(8,128)(2,1)S(1)}, bf16[4,128,128]{2,1,0:T(8,128)(2,1)}, u32[]{:S(2)}) copy-start(bf16[4,128,128]{2,1,0:T(8,128)(2,1)} %copy.244) | copy-start | bytes 393220
  584.0 28.5 %copy-start.89 = (f32[128,1,128]{2,0,1:T(8,128)S(1)}, f32[128,1,128]{2,0,1:T(8,128)}, u32[]{:S(2)}) copy-start(f32[128,1,128]{2,0,1:T(8,128)} %scatter-add.59) | copy-start | bytes 196612
  584.0 28.6 %copy-start.35 = (bf16[4,128,128]{2,1,0:T(8,128)(2,1)S(1)}, bf16[4,128,128]{2,1,0:T(8,128)(2,1)}, u32[]{:S(2)}) copy-start(bf16[4,128,128]{2,1,0:T(8,128)(2,1)} %copy.249) | copy-start | bytes 393220
  585.2 27.3 %copy-start.109 = (bf16[1,512,32,1]{1,3,2,0:T(2,128)(2,1)S(1)}, bf16[1,512,32,1]{1,3,2,0:T(2,128)(2,1)}, u32[]{:S(2)}) copy-start(bf16[1,512,32,1]{1,3,2,0:T(2,128)(2,1)} %slice.871) | copy-start | bytes 98308
  585.2 27.5 %copy-start.107 = (bf16[1,512,48,1]{1,3,2,0:T(2,128)(2,1)S(1)}, bf16[1,512,48,1]{1,3,2,0:T(2,128)(2,1)}, u32[]{:S(2)}) copy-start(bf16[1,512,48,1]{1,3,2,0:T(2,128)(2,1)} %slice.873) | copy-start | bytes 147460
  585.2 27.6 %copy-start.45 = (bf16[4,128,128]{2,1,0:T(8,128)(2,1)S(1)}, bf16[4,128,128]{2,1,0:T(8,128)(2,1)}, u32[]{:S(2)}) copy-start(bf16[4,128,128]{2,1,0:T(8,128)(2,1)} %copy.254) | copy-start | bytes 393220
  585.2 27.6 %copy-start.103 = (bf16[1,512,64,1]{1,3,2,0:T(2,128)(2,1)S(1)}, bf16[1,512,64,1]{1,3,2,0:T(2,128)(2,1)}, u32[]{:S(2)}) copy-start(bf16[1,512,64,1]{1,3,2,0:T(2,128)(2,1)} %slice.875) | copy-start | bytes 196612
  585.2 27.8 %copy-start.43 = (bf16[4,128,128]{2,1,0:T(8,128)(2,1)S(1)}, bf16[4,128,128]{2,1,0:T(8,128)(2,1)}, u32[]{:S(2)}) copy-start(bf16[4,128,128]{2,1,0:T(8,128)(2,1)} %copy.259) | copy-start | bytes 393220
  585.2 27.8 %copy-start.102 = (bf16[1,512,80,1]{1,3,2,0:T(2,128)(2,1)S(1)}, bf16[1,512,80,1]{1,3,2,0:T(2,128)(2,1)}, u32[]{:S(2)}) copy-start(bf16[1,512,80,1]{1,3,2,0:T(2,128)(2,1)} %slice.877) | copy-start | bytes 245764
  585.2 28.0 %all-to-all-start.6 = ((f32[32,4,128]{2,1,0:T(4,128)}), f32[32,4,128]{2,1,0:T(4,128)S(1)}, u32[]{:S(2)}, u32[]{:S(2)}) async-start(f32[32,4,128]{2,1,0:T(4,128)} %bitcast.980), calls=%async_computation.6 | async-start | bytes 131072 | tf_op jit(solution)/shard_map/all_to_all | solution.py:134
  610.4 13.3 %copy-start.41 = (bf16[4,128,128]{2,1,0:T(8,128)(2,1)S(1)}, bf16[4,128,128]{2,1,0:T(8,128)(2,1)}, u32[]{:S(2)}) copy-start(bf16[4,128,128]{2,1,0:T(8,128)(2,1)} %copy.264) | copy-start | bytes 393220
  610.4 14.4 %copy-start.84 = (bf16[4,128,128]{2,1,0:T(8,128)(2,1)S(1)}, bf16[4,128,128]{2,1,0:T(8,128)(2,1)}, u32[]{:S(2)}) copy-start(bf16[4,128,128]{2,1,0:T(8,128)(2,1)} %copy.230) | copy-start | bytes 393220
  610.4 14.4 %copy-start.88 = (f32[128,1,128]{2,0,1:T(8,128)S(1)}, f32[128,1,128]{2,0,1:T(8,128)}, u32[]{:S(2)}) copy-start(f32[128,1,128]{2,0,1:T(8,128)} %scatter-add.46) | copy-start | bytes 196612
  612.3 13.6 %copy-start.39 = (bf16[4,128,128]{2,1,0:T(8,128)(2,1)S(1)}, bf16[4,128,128]{2,1,0:T(8,128)(2,1)}, u32[]{:S(2)}) copy-start(bf16[4,128,128]{2,1,0:T(8,128)(2,1)} %copy.269) | copy-start | bytes 393220
  612.5 14.7 %copy-start.69 = (bf16[4,128,128]{2,1,0:T(8,128)(2,1)S(1)}, bf16[4,128,128]{2,1,0:T(8,128)(2,1)}, u32[]{:S(2)}) copy-start(bf16[4,128,128]{2,1,0:T(8,128)(2,1)} %copy.231) | copy-start | bytes 393220
  612.8 15.5 %copy-start.81 = (bf16[4,128,128]{2,1,0:T(8,128)(2,1)S(1)}, bf16[4,128,128]{2,1,0:T(8,128)(2,1)}, u32[]{:S(2)}) copy-start(bf16[4,128,128]{2,1,0:T(8,128)(2,1)} %copy.232) | copy-start | bytes 393220
  613.2 16.4 %copy-start.77 = (bf16[4,128,128]{2,1,0:T(8,128)(2,1)S(1)}, bf16[4,128,128]{2,1,0:T(8,128)(2,1)}, u32[]{:S(2)}) copy-start(bf16[4,128,128]{2,1,0:T(8,128)(2,1)} %copy.233) | copy-start | bytes 393220
  613.2 17.6 %copy-start.73 = (bf16[4,128,128]{2,1,0:T(8,128)(2,1)S(1)}, bf16[4,128,128]{2,1,0:T(8,128)(2,1)}, u32[]{:S(2)}) copy-start(bf16[4,128,128]{2,1,0:T(8,128)(2,1)} %copy.234) | copy-start | bytes 393220
  613.2 17.6 %copy-start.111 = (bf16[96,1,1,128]{3,1,0,2:T(2,128)(2,1)S(1)}, bf16[96,1,1,128]{3,1,0,2:T(2,128)(2,1)}, u32[]{:S(2)}) copy-start(bf16[96,1,1,128]{3,1,0,2:T(2,128)(2,1)} %slice.863) | copy-start | bytes 73732
  613.2 18.9 %copy-start.65 = (bf16[4,128,128]{2,1,0:T(8,128)(2,1)S(1)}, bf16[4,128,128]{2,1,0:T(8,128)(2,1)}, u32[]{:S(2)}) copy-start(bf16[4,128,128]{2,1,0:T(8,128)(2,1)} %copy.235) | copy-start | bytes 393220
  613.8 34.8 %all-to-all-start.4 = ((bf16[32,128,128]{2,1,0:T(8,128)(2,1)}), bf16[32,128,128]{2,1,0:T(8,128)(2,1)S(1)}, u32[]{:S(2)}, u32[]{:S(2)}) async-start(bf16[32,128,128]{2,1,0:T(8,128)(2,1)} %bitcast.969), calls=%async_computation.4 | async-start | bytes 2097152 | tf_op jit(solution)/shard_map/all_to_all | solution.py:124
  623.6 8.8 %copy-start.37 = (bf16[4,128,128]{2,1,0:T(8,128)(2,1)S(1)}, bf16[4,128,128]{2,1,0:T(8,128)(2,1)}, u32[]{:S(2)}) copy-start(bf16[4,128,128]{2,1,0:T(8,128)(2,1)} %copy.274) | copy-start | bytes 393220
  623.6 33.3 %copy-start.55 = (bf16[4,128,128]{2,1,0:T(8,128)(2,1)S(1)}, bf16[4,128,128]{2,1,0:T(8,128)(2,1)}, u32[]{:S(2)}) copy-start(bf16[4,128,128]{2,1,0:T(8,128)(2,1)} %copy.236) | copy-start | bytes 393220
  626.0 31.0 %copy-start.108 = (bf16[128,1,1,128]{3,1,0,2:T(2,128)(2,1)S(1)}, bf16[128,1,1,128]{3,1,0,2:T(2,128)(2,1)}, u32[]{:S(2)}) copy-start(bf16[128,1,1,128]{3,1,0,2:T(2,128)(2,1)} %slice.868) | copy-start | bytes 98308
  626.0 31.0 %copy-start.129 = (f32[512]{0:T(512)S(1)}, f32[512]{0:T(512)}, u32[]{:S(2)}) copy-start(f32[512]{0:T(512)} %copy-done.128) | copy-start | bytes 6148
  632.1 48.9 %copy-start.106 = (f32[32,4,128]{2,1,0:T(4,128)S(1)}, f32[32,4,128]{2,1,0:T(4,128)}, u32[]{:S(2)}) copy-start(f32[32,4,128]{2,1,0:T(4,128)} %copy-done.105) | copy-start | bytes 196612
  632.1 49.6 %copy-start.1 = (bf16[128,1024]{1,0:T(8,128)(2,1)S(1)}, bf16[128,1024]{1,0:T(8,128)(2,1)}, u32[]{:S(2)}) copy-start(bf16[128,1024]{1,0:T(8,128)(2,1)} %param.42) | copy-start | bytes 786436
  648.6 18.0 %all-to-all-start.8 = ((f32[32,4,128]{2,1,0:T(4,128)}), f32[32,4,128]{2,1,0:T(4,128)S(1)}, u32[]{:S(2)}, u32[]{:S(2)}) async-start(f32[32,4,128]{2,1,0:T(4,128)} %bitcast.242), calls=%async_computation.9 | async-start | bytes 131072 | tf_op jit(solution)/shard_map/all_to_all | solution.py:136
  666.7 13.7 %all-to-all-start.7 = ((f32[32,4,128]{2,1,0:T(4,128)}), f32[32,4,128]{2,1,0:T(4,128)S(1)}, u32[]{:S(2)}, u32[]{:S(2)}) async-start(f32[32,4,128]{2,1,0:T(4,128)} %bitcast.204), calls=%async_computation.8 | async-start | bytes 131072 | tf_op jit(solution)/shard_map/all_to_all | solution.py:135
  (132 other events, 530.5 us)
Sparse Core Ops, SparseCore 0:
  556.3 43.1 reduce-scatter.1
